TPU v7x, 512 devices: a whole 4x4x16 slice. The times are simulated.
512 devices in a mesh: expert: 4 (over z_hi, core), rep: 4 (over y), hid: 32 (over x, z_lo).
Axes of the slice: x: 4, y: 4, z: 16 (z_hi: 2, z_lo: 8; z = z_hi * 8 + z_lo), core: 2. Of those that a mesh axis runs over, the one named last changes fastest.
Arguments:
- tokens: bfloat16 [1024, 6144], P(('expert', 'hid'), 'rep'), may hold values from -6 to 6
- norm_gain: float32 [6144], P('rep'), may hold values from 0.25 to 1.75
- expert_ids: int32 [1024, 2], P(('expert', 'hid')), may hold values from 0 to 3, as said below
- slot_ids: int32 [1024, 2], P(('expert', 'hid')), may hold values from 0 to 4, as said below
- w_gate: bfloat16 [4, 6144, 8192], P('expert', 'rep', 'hid'), may hold values from -0.078125 to 0.078125
- w_up: bfloat16 [4, 6144, 8192], P('expert', 'rep', 'hid'), may hold values from -0.078125 to 0.078125
- grad_gate: bfloat16 [4, 640, 8192], P('expert', None, 'hid'), may hold values from -1.1953125 to 1.1953125
- grad_up: bfloat16 [4, 640, 8192], P('expert', None, 'hid'), may hold values from -1.1953125 to 1.1953125
Outputs:
- grad_w_gate: bfloat16 [4, 6144, 8192], P('expert', 'rep', 'hid')
- grad_w_up: bfloat16 [4, 6144, 8192], P('expert', 'rep', 'hid')
- grad_tokens: bfloat16 [1024, 6144], P(('expert', 'hid'), 'rep')
Inputs may be any that keep to these rules, and one draw needn't show every extreme that they name: `expert_ids`: each token names two different experts; among the 8 tokens of one block, no expert is named more than 5 times and some expert exactly 5 times. Within one block of 8 tokens, the pairs (expert_ids[t, k], slot_ids[t, k]) are all different.
All inputs are finite; a program needn't handle non-finite values.
Results may differ from a plain program's by a relative error of at most 0.0049.
Values may be sent and summed in bfloat16 or wider, within the bound.
No kernel may reach another device: no remote copies, remote signals or barrier semaphores. Data moves between devices by JAX's collectives and lax.ppermute only.
A program may use at most 64 MiB of HBM per device.

v0:
```python
import jax
import jax.numpy as jnp
from jax import lax
from jax.sharding import PartitionSpec as P

D = 6144


def copy_for_each(x, axis):
    size = lax.axis_size(axis)
    return lax.all_to_all(jnp.broadcast_to(x[None], (size, *x.shape)), axis, 0, 0, tiled=True)


def of_everyone(x, axis):
    return copy_for_each(x, axis).sum(axis=0)


def feature_total(partial_value):
    return of_everyone(partial_value, "rep")


def on_device(tokens, norm_gain, expert_ids, slot_ids, w_gate, w_up, grad_gate, grad_up):
    groups = lax.axis_size("expert")
    block_tokens = tokens.shape[0]
    slot_count = 5 * block_tokens // (2 * groups)
    values = tokens.astype(jnp.float32)
    square_sums = feature_total(jnp.sum(values * values, axis=1))
    inverse_rms = lax.rsqrt(square_sums / D + 1e-05)[:, None]
    scaled_in = values * inverse_rms
    normed = (scaled_in * norm_gain).astype(jnp.bfloat16)
    slot_code = expert_ids * slot_count + slot_ids
    codes_all = jnp.arange(groups * slot_count, dtype=jnp.int32)
    onehot = (
        (slot_code[:, 0][None, :] == codes_all[:, None])
        | (slot_code[:, 1][None, :] == codes_all[:, None])
    ).astype(jnp.bfloat16)
    feat_width = normed.shape[1]
    outgoing = (
        jnp.dot(onehot, normed, preferred_element_type=jnp.float32)
        .astype(jnp.bfloat16)
        .reshape(groups, slot_count, feat_width)
    )
    arrived = lax.all_to_all(outgoing, "expert", split_axis=0, concat_axis=0, tiled=True)
    own_rows = arrived.reshape(groups * slot_count, feat_width)
    gate_cot = grad_gate[0]
    up_cot = grad_up[0]
    row_contract = (((0,), (0,)), ((), ()))
    gathered = lax.all_gather(own_rows, "hid", axis=0, tiled=True)
    gate_part = gate_cot
    up_part = up_cot
    new_gate = lax.dot_general(
        gathered, gate_part, row_contract, preferred_element_type=jnp.float32
    )
    new_up = lax.dot_general(gathered, up_part, row_contract, preferred_element_type=jnp.float32)
    unit_contract = (((1,), (1,)), ((), ()))
    gate_part = gate_cot
    up_part = up_cot
    first_term = lax.dot_general(
        gate_part, w_gate[0], unit_contract, preferred_element_type=jnp.float32
    )
    summed = lax.psum_scatter(
        first_term
        + lax.dot_general(up_part, w_up[0], unit_contract, preferred_element_type=jnp.float32),
        "hid",
        scatter_dimension=0,
        tiled=True,
    )
    returned_rows = lax.all_to_all(
        summed.astype(jnp.bfloat16).reshape(groups, slot_count, feat_width),
        "expert",
        split_axis=0,
        concat_axis=0,
        tiled=True,
    )
    normed_grad = jnp.dot(
        onehot.T,
        returned_rows.reshape(groups * slot_count, feat_width),
        preferred_element_type=jnp.float32,
    )
    scaled = normed_grad * norm_gain
    dotted = feature_total(jnp.sum(scaled * scaled_in, axis=1)) / D
    grad_tokens = (inverse_rms * (scaled - scaled_in * dotted[:, None])).astype(jnp.bfloat16)
    return (new_gate.astype(jnp.bfloat16)[None], new_up.astype(jnp.bfloat16)[None], grad_tokens)


def solution(mesh):
    placed = (
        P(("expert", "hid"), "rep"),
        P("rep"),
        P(("expert", "hid"), None),
        P(("expert", "hid"), None),
        P("expert", "rep", "hid"),
        P("expert", "rep", "hid"),
        P("expert", None, "hid"),
        P("expert", None, "hid"),
    )
    return jax.shard_map(
        on_device,
        mesh=mesh,
        in_specs=placed,
        out_specs=(
            P("expert", "rep", "hid"),
            P("expert", "rep", "hid"),
            P(("expert", "hid"), "rep"),
        ),
        check_vma=False,
    )
```

profile of v0, /device:TPU:8, one launch (start us, length us, event | category | flops | bytes accessed | tf_op | source)
XLA Modules:
  0.0 289.3 jit_solution(9607621341677522654)
XLA Ops:
  7.2 0.0 copy-start
  7.2 0.9 fusion.18
  8.1 0.6 broadcast_in_dim.8
  8.7 9.0 %all-to-all-start = ((f32[4,1,8]{2,1,0:T(1,128)}), f32[4,1,8]{2,1,0:T(1,128)S(1)}, u32[]{:S(2)}, u32[]{:S(2)}) async-start(f32[4,1,8]{2,1,0:T(1,128)} %broadcast_in_dim.8), calls=%async_computation | async-start | bytes 4096 | tf_op jit(solution)/shard_map/all_to_all | solution.py:11
  17.7 0.0 copy-done
  17.7 0.0 copy-start.5
  17.7 0.0 copy-start.1
  17.7 0.0 copy-start.4
  17.7 3.6 %fusion.4 = f32[640,1536]{1,0:T(8,128)} fusion(bf16[1,1536,256]{2,1,0:T(8,128)(2,1)S(1)} %copy-done, bf16[1,640,256]{2,1,0:T(8,128)(2,1)} %param.14), kind=kOutput, calls=%fused_computation.8 | convolution fusion | flops 503316480 | bytes 5046272 | tf_op jit(solution)/shard_map/dot_general | solution.py:58
  21.4 0.0 copy-done.6
  21.4 0.0 copy-done.7
  21.4 0.0 all-to-all-done
  21.5 0.0 copy-done.2
  21.5 0.0 copy-done.5
  21.5 0.2 convolution_convert_fusion.2
  21.7 0.7 reshape.41
  22.4 11.0 %all-to-all-start.1 = ((bf16[4,5,1536]{2,1,0:T(8,128)(2,1)}), bf16[4,5,1536]{2,1,0:T(8,128)(2,1)S(1)}, u32[]{:S(2)}, u32[]{:S(2)}) async-start(bf16[4,5,1536]{2,1,0:T(8,128)(2,1)} %reshape.41), calls=%async_computation.1 | async-start | bytes 196608 | tf_op jit(solution)/shard_map/all_to_all | solution.py:43
  33.4 0.0 all-gather.3.cloned.1.call-start
  33.4 0.0 copy-done.1
  33.4 0.0 copy-done.4
  33.4 4.7 %convolution_add_fusion = f32[640,1536]{1,0:T(8,128)} fusion(f32[640,1536]{1,0:T(8,128)} %fusion.4, bf16[1,1536,256]{2,1,0:T(8,128)(2,1)S(1)} %copy-done.1, bf16[1,640,256]{2,1,0:T(8,128)(2,1)S(1)} %copy-done.4), kind=kOutput, calls=%fused_computation | convolution fusion | flops 504299520 | bytes 8978432 | tf_op jit(solution)/shard_map/dot_general | solution.py:63
  38.1 8.4 %all-to-all-done.1 = bf16[4,5,1536]{2,1,0:T(8,128)(2,1)S(1)} async-done(((bf16[4,5,1536]{2,1,0:T(8,128)(2,1)}), bf16[4,5,1536]{2,1,0:T(8,128)(2,1)S(1)}, u32[]{:S(2)}, u32[]{:S(2)}) %all-to-all-start.1) | async-done | bytes 61472 | tf_op jit(solution)/shard_map/all_to_all | solution.py:43
  46.5 0.7 reshape.45
  47.1 0.0 all-gather.3.cloned.1.call-update
  47.1 160.0 %fusion = f32[24,1536]{1,0:T(8,128)S(1)} fusion(f32[640,1536]{1,0:T(8,128)} %convolution_add_fusion), kind=kCustom, calls=%all-reduce-scatter | all-reduce-scatter fusion | flops 1179649 | bytes 4081664
  207.1 1.3 collective-permute-start.5
  208.5 1.3 collective-permute-start
  209.8 1.3 collective-permute-start.1
  211.1 1.3 collective-permute-start.2
  212.4 8.9 %collective-permute-start.3 = (bf16[24,1536]{1,0:T(8,128)(2,1)S(1)}, bf16[24,1536]{1,0:T(8,128)(2,1)S(1)}, u32[]{:S(2)}, u32[]{:S(2)}) collective-permute-start(bf16[24,1536]{1,0:T(8,128)(2,1)S(1)} %convert.10), channel_id=1, source_target_pairs={{0,4},{1,5},{2,6},{3,7},{4,8},{5,9},{6,10},{7,11},{8,12},{9,13},{1... | collective-permute-start | bytes 221192
  221.2 0.0 collective-permute-done.5
  221.3 1.3 collective-permute-start.4
  222.6 1.3 dynamic-slice.4
  224.5 0.0 collective-permute-done
  224.5 0.0 collective-permute-done.1
  224.5 0.0 collective-permute-done.2
  224.5 0.0 collective-permute-done.3
  224.5 0.0 collective-permute-done.4
  224.5 1.1 concatenate
  225.7 21.8 %all_to_all.22 = bf16[4,5,1536]{2,1,0:T(8,128)(2,1)S(1)} all-to-all(bf16[4,5,1536]{2,1,0:T(8,128)(2,1)S(1)} %reshape.43), channel_id=1, replica_groups=mesh['expert'=4,'rep'=4,'hid'=32] {'expert'}, dimensions={0} | all-to-all | bytes 122880 | tf_op jit(solution)/shard_map/all_to_all | solution.py:68
  247.6 0.3 fusion.14
  247.9 8.3 %all_to_all.23 = f32[4,1,8]{2,1,0:T(1,128)S(1)} all-to-all(f32[4,1,8]{2,1,0:T(1,128)S(1)} %broadcast_in_dim.11), channel_id=1, replica_groups=mesh['expert'=4,'rep'=4,'hid'=32] {'rep'}, dimensions={0} | all-to-all | bytes 256 | tf_op jit(solution)/shard_map/all_to_all | solution.py:11
  256.2 0.7 fusion.17
  256.9 19.5 %all-gather.3.cloned.1.call-done = bf16[32,20,1536]{2,1,0:T(8,128)(2,1)} async-done(((bf16[1,20,1536]{2,1,0:T(8,128)(2,1)}), bf16[32,20,1536]{2,1,0:T(8,128)(2,1)}) %all-gather.3.cloned.1.call-update) | async-done | bytes 1966096 | tf_op jit(solution)/shard_map/all_gather | solution.py:48
  276.4 2.6 reshape.46
  279.0 0.0 copy-done.3
  279.0 1.7 fusion.1
  280.7 1.7 fusion.2
  (16 shorter events, 0.2 us)
Async XLA Ops:
  7.2 10.5 %copy-start = (bf16[1,1536,256]{2,1,0:T(8,128)(2,1)S(1)}, bf16[1,1536,256]{2,1,0:T(8,128)(2,1)}, u32[]{:S(2)}) copy-start(bf16[1,1536,256]{2,1,0:T(8,128)(2,1)} %param.12) | copy-start | bytes 2359300
  8.7 12.7 %all-to-all-start = ((f32[4,1,8]{2,1,0:T(1,128)}), f32[4,1,8]{2,1,0:T(1,128)S(1)}, u32[]{:S(2)}, u32[]{:S(2)}) async-start(f32[4,1,8]{2,1,0:T(1,128)} %broadcast_in_dim.8), calls=%async_computation | async-start | bytes 4096 | tf_op jit(solution)/shard_map/all_to_all | solution.py:11
  17.7 3.7 %copy-start.6 = (s32[8,2]{0,1:T(2,128)S(1)}, s32[8,2]{0,1:T(2,128)}, u32[]{:S(2)}) copy-start(s32[8,2]{0,1:T(2,128)} %param.11) | copy-start | bytes 196
  17.7 3.7 %copy-start.7 = (s32[8,2]{0,1:T(2,128)S(1)}, s32[8,2]{0,1:T(2,128)}, u32[]{:S(2)}) copy-start(s32[8,2]{0,1:T(2,128)} %param.10) | copy-start | bytes 196
  17.7 3.8 %copy-start.2 = (bf16[8,1536]{1,0:T(8,128)(2,1)S(1)}, bf16[8,1536]{1,0:T(8,128)(2,1)}, u32[]{:S(2)}) copy-start(bf16[8,1536]{1,0:T(8,128)(2,1)} %param.8) | copy-start | bytes 73732
  17.7 3.8 %copy-start.5 = (f32[1536]{0:T(1024)S(1)}, f32[1536]{0:T(1024)}, u32[]{:S(2)}) copy-start(f32[1536]{0:T(1024)} %param.9) | copy-start | bytes 18436
  17.7 15.7 %copy-start.1 = (bf16[1,1536,256]{2,1,0:T(8,128)(2,1)S(1)}, bf16[1,1536,256]{2,1,0:T(8,128)(2,1)}, u32[]{:S(2)}) copy-start(bf16[1,1536,256]{2,1,0:T(8,128)(2,1)} %param.13) | copy-start | bytes 2359300
  17.7 15.7 %copy-start.4 = (bf16[1,640,256]{2,1,0:T(8,128)(2,1)S(1)}, bf16[1,640,256]{2,1,0:T(8,128)(2,1)}, u32[]{:S(2)}) copy-start(bf16[1,640,256]{2,1,0:T(8,128)(2,1)} %param.15) | copy-start | bytes 983044
  22.4 24.1 %all-to-all-start.1 = ((bf16[4,5,1536]{2,1,0:T(8,128)(2,1)}), bf16[4,5,1536]{2,1,0:T(8,128)(2,1)S(1)}, u32[]{:S(2)}, u32[]{:S(2)}) async-start(bf16[4,5,1536]{2,1,0:T(8,128)(2,1)} %reshape.41), calls=%async_computation.1 | async-start | bytes 196608 | tf_op jit(solution)/shard_map/all_to_all | solution.py:43
  33.4 243.1 %all-gather.3.cloned.1.call-start = ((), (), s32[]{:S(2)}) async-start(), calls=%async_computation.4 | async-start | bytes 2433024 | tf_op jit(solution)/shard_map/all_gather | solution.py:48
  207.1 14.1 %collective-permute-start.5 = (bf16[4,1536]{1,0:T(4,128)(2,1)S(1)}, bf16[4,1536]{1,0:T(4,128)(2,1)S(1)}, u32[]{:S(2)}, u32[]{:S(2)}) collective-permute-start(bf16[4,1536]{1,0:T(4,128)(2,1)S(1)} %slice.8), channel_id=1, source_target_pairs={{0,6},{1,7},{2,8},{3,9},{4,10},{5,11},{6,12},{7,13},{8,14},{9,15},... | collective-permute-start | bytes 36872
  208.5 16.0 %collective-permute-start = (bf16[24,1536]{1,0:T(8,128)(2,1)S(1)}, bf16[24,1536]{1,0:T(8,128)(2,1)S(1)}, u32[]{:S(2)}, u32[]{:S(2)}) collective-permute-start(bf16[24,1536]{1,0:T(8,128)(2,1)S(1)} %convert.10), channel_id=1, source_target_pairs={{0,1},{1,2},{2,3},{3,4},{4,5},{5,6},{6,7},{7,8},{8,9},{9,10},{10,1... | collective-permute-start | bytes 221192
  209.8 14.7 %collective-permute-start.1 = (bf16[24,1536]{1,0:T(8,128)(2,1)S(1)}, bf16[24,1536]{1,0:T(8,128)(2,1)S(1)}, u32[]{:S(2)}, u32[]{:S(2)}) collective-permute-start(bf16[24,1536]{1,0:T(8,128)(2,1)S(1)} %convert.10), channel_id=1, source_target_pairs={{0,2},{1,3},{2,4},{3,5},{4,6},{5,7},{6,8},{7,9},{8,10},{9,11},{10,... | collective-permute-start | bytes 221192
  211.1 13.4 %collective-permute-start.2 = (bf16[24,1536]{1,0:T(8,128)(2,1)S(1)}, bf16[24,1536]{1,0:T(8,128)(2,1)S(1)}, u32[]{:S(2)}, u32[]{:S(2)}) collective-permute-start(bf16[24,1536]{1,0:T(8,128)(2,1)S(1)} %convert.10), channel_id=1, source_target_pairs={{0,3},{1,4},{2,5},{3,6},{4,7},{5,8},{6,9},{7,10},{8,11},{9,12},{10... | collective-permute-start | bytes 221192
  212.4 12.1 %collective-permute-start.3 = (bf16[24,1536]{1,0:T(8,128)(2,1)S(1)}, bf16[24,1536]{1,0:T(8,128)(2,1)S(1)}, u32[]{:S(2)}, u32[]{:S(2)}) collective-permute-start(bf16[24,1536]{1,0:T(8,128)(2,1)S(1)} %convert.10), channel_id=1, source_target_pairs={{0,4},{1,5},{2,6},{3,7},{4,8},{5,9},{6,10},{7,11},{8,12},{9,13},{1... | collective-permute-start | bytes 221192
  221.3 3.3 %collective-permute-start.4 = (bf16[24,1536]{1,0:T(8,128)(2,1)S(1)}, bf16[24,1536]{1,0:T(8,128)(2,1)S(1)}, u32[]{:S(2)}, u32[]{:S(2)}) collective-permute-start(bf16[24,1536]{1,0:T(8,128)(2,1)S(1)} %convert.10), channel_id=1, source_target_pairs={{0,5},{1,6},{2,7},{3,8},{4,9},{5,10},{6,11},{7,12},{8,13},{9,14},{... | collective-permute-start | bytes 221192
  247.5 31.5 %copy-start.3 = (bf16[1,640,256]{2,1,0:T(8,128)(2,1)S(1)}, bf16[1,640,256]{2,1,0:T(8,128)(2,1)}, u32[]{:S(2)}) copy-start(bf16[1,640,256]{2,1,0:T(8,128)(2,1)} %param.14) | copy-start | bytes 983044
Sparse Core Ops, SparseCore 0:
  47.3 229.1 all-gather.2
where the time goes:
time: 290 us; the launch traced here: 289 us
  blocking collectives  190 us (66%)
  starting transfers between devices  35.3 us (12%)
  waiting for transfers between devices  28 us (10%)
  between operations  14.9 us (5%)
  matrix products  12.3 us (4%)
  local copies, waits for them, and re-layouts  7.02 us (2%)
    unnamed x1, blocking collectives  160 us
    all_to_all x1, blocking collectives, on_device(): lax.all_to_all(summed.astype(jnp.bfloat16).reshape(groups, slot_count, fe...  21.8 us
    all_gather x1, waiting for transfers between devices, on_device(): gathered = lax.all_gather(own_rows, 'hid', axis=0, tiled=True)  19.5 us
    unnamed x6, starting transfers between devices  15.3 us
    all_to_all x1, starting transfers between devices, on_device(): lax.all_to_all(outgoing, 'expert', split_axis=0, concat_axis=0, tiled=True)  11 us
    all_to_all x1, starting transfers between devices, copy_for_each(): lax.all_to_all(jnp.broadcast_to(x[None], (size, *x.shape)), axis, 0, 0, t...  8.98 us
    all_to_all x1, waiting for transfers between devices, on_device(): lax.all_to_all(outgoing, 'expert', split_axis=0, concat_axis=0, tiled=True)  8.38 us
    all_to_all x1, blocking collectives, copy_for_each(): lax.all_to_all(jnp.broadcast_to(x[None], (size, *x.shape)), axis, 0, 0, t...  8.3 us
  transfers between devices with their start and end apart: 9, of which 2 were waited for; matrix products, arithmetic and copies ran while one was open for 59% of the time, Pallas kernels for 0%

commit v1 on v0

v1 whole, which is shorter than its diff:
```python
import jax
import jax.numpy as jnp
from jax import lax
from jax.sharding import Mesh
from jax.sharding import PartitionSpec as P

D = 6144
CAP = 5
TOK = 8
RING = ("zh", "zl")
LANES = 128


def exchange(x, axis):
    return lax.all_to_all(x, axis, 0, 0, tiled=True)


def copy_for_each(x, axis):
    size = lax.axis_size(axis)
    return exchange(jnp.broadcast_to(x[None], (size, *x.shape)), axis)


def feature_total(partial_value):
    return copy_for_each(partial_value[None], "rep").sum(axis=(0, 1))


def swap_cores(x):
    return lax.ppermute(x, "core", [(0, 1), (1, 0)])


def on_device(tokens, norm_gain, expert_ids, slot_ids, w_gate, w_up, grad_gate, grad_up):
    zh_n, core_n, x_n, zl_n = (lax.axis_size(a) for a in ("zh", "core", "x", "zl"))
    ring_n = zh_n * zl_n
    line_tokens = ring_n * TOK
    line_rows = zl_n * zh_n * core_n * CAP
    width = tokens.shape[1]
    core = lax.axis_index("core")
    mine = lax.axis_index("zh") * core_n + core
    partner = lax.axis_index("zh") * core_n + (1 - core)

    unit_contract = (((1,), (1,)), ((), ()))
    part = lax.dot_general(
        grad_gate[0], w_gate[0], unit_contract, preferred_element_type=jnp.float32
    ) + lax.dot_general(grad_up[0], w_up[0], unit_contract, preferred_element_type=jnp.float32)
    part = part.astype(jnp.bfloat16).reshape(x_n, line_rows, width)

    values = tokens.astype(jnp.float32)
    square_sums = feature_total(jnp.sum(values * values, axis=1))
    inverse_rms = lax.rsqrt(square_sums / D + 1e-05)[:, None]
    scaled_in = values * inverse_rms
    normed = (scaled_in * norm_gain).astype(jnp.bfloat16)
    code = (expert_ids * CAP + slot_ids).astype(jnp.bfloat16)
    tagged = jnp.concatenate([normed, jnp.pad(code, ((0, 0), (0, LANES - 2)))], axis=1)

    line = copy_for_each(tagged, RING).reshape(line_tokens, width + LANES)
    line_normed = line[:, :width]
    codes = line[:, width : width + 2].astype(jnp.int32)
    token = jnp.arange(line_tokens, dtype=jnp.int32)
    block = token // TOK
    base = (((block % zl_n) * zh_n + block // zl_n) * core_n + core) * CAP

    def rows_of(expert):
        slot = codes - expert * CAP
        return jnp.where((slot >= 0) & (slot < CAP), base[:, None] + slot, -1)

    row = jnp.arange(line_rows, dtype=jnp.int32)

    def choice(expert):
        at = rows_of(expert)
        return ((at[:, 0][:, None] == row[None]) | (at[:, 1][:, None] == row[None])).astype(
            jnp.bfloat16
        )

    to_mine = choice(mine)
    to_partner = choice(partner)
    first = (((0,), (0,)), ((), ()))

    def rows_from(chosen):
        return lax.dot_general(
            chosen, line_normed, first, preferred_element_type=jnp.float32
        ).astype(jnp.bfloat16)

    own_rows = rows_from(to_mine) + swap_cores(rows_from(to_partner))
    gathered = copy_for_each(own_rows, "x").reshape(x_n * line_rows, width)
    new_gate = lax.dot_general(gathered, grad_gate[0], first, preferred_element_type=jnp.float32)
    new_up = lax.dot_general(gathered, grad_up[0], first, preferred_element_type=jnp.float32)

    line_sum = exchange(part, "x").astype(jnp.float32).sum(axis=0).astype(jnp.bfloat16)
    other_sum = swap_cores(line_sum)
    by_token = jnp.dot(to_mine, line_sum, preferred_element_type=jnp.float32) + jnp.dot(
        to_partner, other_sum, preferred_element_type=jnp.float32
    )
    by_token = by_token.astype(jnp.bfloat16).reshape(ring_n, TOK, width)
    normed_grad = exchange(by_token, RING).astype(jnp.float32).sum(axis=0)

    scaled = normed_grad * norm_gain
    dotted = feature_total(jnp.sum(scaled * scaled_in, axis=1)) / D
    grad_tokens = (inverse_rms * (scaled - scaled_in * dotted[:, None])).astype(jnp.bfloat16)
    return (new_gate.astype(jnp.bfloat16)[None], new_up.astype(jnp.bfloat16)[None], grad_tokens)


def solution(mesh):
    physical = Mesh(mesh.devices.reshape(2, 2, 4, 4, 8), ("zh", "core", "rep", "x", "zl"))
    expert, hid = ("zh", "core"), ("x", "zl")
    placed = (
        P(expert + hid, "rep"),
        P("rep"),
        P(expert + hid, None),
        P(expert + hid, None),
        P(expert, "rep", hid),
        P(expert, "rep", hid),
        P(expert, None, hid),
        P(expert, None, hid),
    )
    return jax.shard_map(
        on_device,
        mesh=physical,
        in_specs=placed,
        out_specs=(P(expert, "rep", hid), P(expert, "rep", hid), P(expert + hid, "rep")),
        check_vma=False,
    )
```

time: 290 us -> 151 us (0.52)
  the two profiles are of different devices: /device:TPU:8 before, /device:TPU:32 now
where the time goes in v1:
time: 151 us; the launch traced here: 150 us
  waiting for transfers between devices  87 us (58%)
  starting transfers between devices  44.7 us (30%)
  matrix products  10.4 us (7%)
  local copies, waits for them, and re-layouts  3.94 us (3%)
  other arithmetic  3.32 us (2%)
    all_to_all x6, waiting for transfers between devices, exchange(): return lax.all_to_all(x, axis, 0, 0, tiled=True)  87 us
    all_to_all x6, starting transfers between devices, exchange(): return lax.all_to_all(x, axis, 0, 0, tiled=True)  40.9 us
    ppermute x2, starting transfers between devices, swap_cores(): return lax.ppermute(x, 'core', [(0, 1), (1, 0)])  3.83 us
    broadcast_in_dim x4, local copies, waits for them, and re-layouts, copy_for_each(): return exchange(jnp.broadcast_to(x[None], (size, *x.shape)), axis)  3.39 us
  transfers between devices with their start and end apart: 8, of which 6 were waited for; matrix products, arithmetic and copies ran while one was open for 6% of the time, Pallas kernels for 0%

profile of v1, /device:TPU:32, one launch (start us, length us, event | category | flops | bytes accessed | tf_op | source)
XLA Modules:
  0.0 150.1 jit_solution(519805262474254355)
XLA Ops:
  0.6 0.0 copy-start
  0.6 0.9 fusion.48
  1.6 0.6 broadcast_in_dim.17
  2.2 4.5 %all-to-all-start = ((f32[4,1,8]{2,1,0:T(1,128)}), f32[4,1,8]{2,1,0:T(1,128)S(1)}, u32[]{:S(2)}, u32[]{:S(2)}) async-start(f32[4,1,8]{2,1,0:T(1,128)} %broadcast_in_dim.17), calls=%async_computation | async-start | bytes 4096 | tf_op jit(solution)/shard_map/all_to_all | solution.py:15
  6.6 0.0 copy-done
  6.6 1.8 %fusion.6 = f32[640,1536]{1,0:T(8,128)S(1)} fusion(bf16[1,1536,256]{2,1,0:T(8,128)(2,1)S(1)} %copy-done, bf16[1,640,256]{2,1,0:T(8,128)(2,1)} %param.14), kind=kOutput, calls=%fused_computation.12 | convolution fusion | flops 503316480 | bytes 5046272 | tf_op jit(solution)/shard_map/dot_general | solution.py:42
  8.4 0.0 copy-done.1
  8.4 0.0 copy-done.4
  8.4 2.0 %add_convert_fusion = bf16[640,1536]{1,0:T(8,128)(2,1)} fusion(f32[640,1536]{1,0:T(8,128)S(1)} %fusion.6, bf16[1,1536,256]{2,1,0:T(8,128)(2,1)S(1)} %copy-done.1, bf16[1,640,256]{2,1,0:T(8,128)(2,1)S(1)} %copy-done.4), kind=kOutput, calls=%fused_computation | convolution fusion | flops 505282560 | bytes 7012352 | tf_op jit(solution)/shard_map/dot_general | solution.py:44
  10.4 1.4 all-to-all-done
  11.8 4.4 %all-to-all-start.3 = ((bf16[4,160,1536]{2,1,0:T(8,128)(2,1)}), bf16[4,160,1536]{2,1,0:T(8,128)(2,1)S(1)}, u32[]{:S(2)}, u32[]{:S(2)}) async-start(bf16[4,160,1536]{2,1,0:T(8,128)(2,1)} %bitcast.31), calls=%async_computation.3 | async-start | bytes 3932160 | tf_op jit(solution)/shard_map/all_to_all | solution.py:15
  16.3 0.0 copy-done.6
  16.3 0.1 copy.21
  16.4 0.0 copy-done.7
  16.4 0.1 copy.22
  16.5 0.0 copy-done.2
  16.5 0.0 copy-done.5
  16.5 0.1 fusion.43
  16.6 23.2 %all-to-all-done.3 = bf16[4,160,1536]{2,1,0:T(8,128)(2,1)S(1)} async-done(((bf16[4,160,1536]{2,1,0:T(8,128)(2,1)}), bf16[4,160,1536]{2,1,0:T(8,128)(2,1)S(1)}, u32[]{:S(2)}, u32[]{:S(2)}) %all-to-all-start.3) | async-done | bytes 1966112 | tf_op jit(solution)/shard_map/all_to_all | solution.py:15
  39.8 0.8 broadcast_in_dim.18
  40.6 15.2 %all-to-all-start.1 = ((bf16[16,8,1664]{2,1,0:T(8,128)(2,1)}), bf16[16,8,1664]{2,1,0:T(8,128)(2,1)S(1)}, u32[]{:S(2)}, u32[]{:S(2)}) async-start(bf16[16,8,1664]{2,1,0:T(8,128)(2,1)} %broadcast_in_dim.18), calls=%async_computation.1 | async-start | bytes 851968 | tf_op jit(solution)/shard_map/all_to_all | solution.py:15
  55.8 1.2 reduce_sum.59
  57.0 1.9 %collective-permute-start.1 = (bf16[160,1536]{1,0:T(8,128)(2,1)}, bf16[160,1536]{1,0:T(8,128)(2,1)S(1)}, u32[]{:S(2)}, u32[]{:S(2)}) collective-permute-start(bf16[160,1536]{1,0:T(8,128)(2,1)} %reduce_sum.59), channel_id=1, source_target_pairs={{0,128},{128,0},{1,129},{129,1},{2,130},{130,2},{3,131},{131,3},{4... | collective-permute-start | bytes 1474568 | tf_op jit(solution)/shard_map/ppermute | solution.py:28
  58.9 17.8 %all-to-all-done.1 = bf16[16,8,1664]{2,1,0:T(8,128)(2,1)S(1)} async-done(((bf16[16,8,1664]{2,1,0:T(8,128)(2,1)}), bf16[16,8,1664]{2,1,0:T(8,128)(2,1)S(1)}, u32[]{:S(2)}, u32[]{:S(2)}) %all-to-all-start.1) | async-done | bytes 426016 | tf_op jit(solution)/shard_map/all_to_all | solution.py:15
  76.7 0.1 fusion.28
  76.7 0.2 slice_reduce_fusion.3
  76.9 0.2 slice_reduce_fusion.1
  77.1 1.4 fusion.18
  78.5 0.0 collective-permute-done.1
  78.5 1.1 fusion.4
  79.5 7.7 %all-to-all-start.4 = ((bf16[16,8,1536]{2,1,0:T(8,128)(2,1)}), bf16[16,8,1536]{2,1,0:T(8,128)(2,1)S(1)}, u32[]{:S(2)}, u32[]{:S(2)}) async-start(bf16[16,8,1536]{2,1,0:T(8,128)(2,1)} %fusion.4), calls=%async_computation.4 | async-start | bytes 786432 | tf_op jit(solution)/shard_map/all_to_all | solution.py:15
  87.3 0.4 convolution_convert_fusion.2
  87.7 1.9 %collective-permute-start = (bf16[160,1536]{1,0:T(8,128)(2,1)S(1)}, bf16[160,1536]{1,0:T(8,128)(2,1)S(1)}, u32[]{:S(2)}, u32[]{:S(2)}) collective-permute-start(bf16[160,1536]{1,0:T(8,128)(2,1)S(1)} %convolution_convert_fusion.2), channel_id=1, source_target_pairs={{0,128},{128,0},{1,129},{129,1},{2,130},{130,2},{3,131},{131,3},{4... | collective-permute-start | bytes 1474568 | tf_op jit(solution)/shard_map/ppermute | solution.py:28
  89.6 19.3 %all-to-all-done.4 = bf16[16,8,1536]{2,1,0:T(8,128)(2,1)S(1)} async-done(((bf16[16,8,1536]{2,1,0:T(8,128)(2,1)}), bf16[16,8,1536]{2,1,0:T(8,128)(2,1)S(1)}, u32[]{:S(2)}, u32[]{:S(2)}) %all-to-all-start.4) | async-done | bytes 393248 | tf_op jit(solution)/shard_map/all_to_all | solution.py:15
  108.9 0.1 convert_reduce_fusion
  109.0 0.2 fusion.44
  109.2 0.6 broadcast_in_dim.23
  109.8 5.3 %all-to-all-start.5 = ((f32[4,1,8]{2,1,0:T(1,128)}), f32[4,1,8]{2,1,0:T(1,128)S(1)}, u32[]{:S(2)}, u32[]{:S(2)}) async-start(f32[4,1,8]{2,1,0:T(1,128)} %broadcast_in_dim.23), calls=%async_computation.5 | async-start | bytes 4096 | tf_op jit(solution)/shard_map/all_to_all | solution.py:15
  115.0 0.0 collective-permute-done
  115.1 0.4 fusion.3
  115.5 4.8 %all-to-all-done.5 = f32[4,1,8]{2,1,0:T(1,128)S(1)} async-done(((f32[4,1,8]{2,1,0:T(1,128)}), f32[4,1,8]{2,1,0:T(1,128)S(1)}, u32[]{:S(2)}, u32[]{:S(2)}) %all-to-all-start.5) | async-done | bytes 160 | tf_op jit(solution)/shard_map/all_to_all | solution.py:15
  120.3 1.4 broadcast_in_dim.20
  121.7 3.7 %all-to-all-start.2 = ((bf16[4,160,1536]{2,1,0:T(8,128)(2,1)}), bf16[4,160,1536]{2,1,0:T(8,128)(2,1)S(1)}, u32[]{:S(2)}, u32[]{:S(2)}) async-start(bf16[4,160,1536]{2,1,0:T(8,128)(2,1)} %broadcast_in_dim.20), calls=%async_computation.2 | async-start | bytes 3932160 | tf_op jit(solution)/shard_map/all_to_all | solution.py:15
  125.5 0.7 fusion.47
  126.1 20.5 %all-to-all-done.2 = bf16[4,160,1536]{2,1,0:T(8,128)(2,1)S(1)} async-done(((bf16[4,160,1536]{2,1,0:T(8,128)(2,1)}), bf16[4,160,1536]{2,1,0:T(8,128)(2,1)S(1)}, u32[]{:S(2)}, u32[]{:S(2)}) %all-to-all-start.2) | async-done | bytes 1966112 | tf_op jit(solution)/shard_map/all_to_all | solution.py:15
  146.7 0.0 copy-done.3
  146.7 1.7 %fusion = bf16[1,1536,256]{2,1,0:T(8,128)(2,1)} fusion(bf16[640,1536]{1,0:T(8,128)(2,1)S(1)} %bitcast.35, bf16[1,640,256]{2,1,0:T(8,128)(2,1)S(1)} %copy-done.3), kind=kOutput, calls=%fused_computation.4 | convolution fusion | flops 503709696 | bytes 3080192 | tf_op jit(solution)/shard_map/dot_general | solution.py:85
  148.4 1.7 %fusion.1 = bf16[1,1536,256]{2,1,0:T(8,128)(2,1)} fusion(bf16[640,1536]{1,0:T(8,128)(2,1)S(1)} %bitcast.36, bf16[1,640,256]{2,1,0:T(8,128)(2,1)S(1)} %copy-done.4), kind=kOutput, calls=%fused_computation.5 | convolution fusion | flops 503709696 | bytes 3080192 | tf_op jit(solution)/shard_map/dot_general | solution.py:86
  (14 shorter events, 0.1 us)
Async XLA Ops:
  0.6 6.0 %copy-start = (bf16[1,1536,256]{2,1,0:T(8,128)(2,1)S(1)}, bf16[1,1536,256]{2,1,0:T(8,128)(2,1)}, u32[]{:S(2)}) copy-start(bf16[1,1536,256]{2,1,0:T(8,128)(2,1)} %param.12) | copy-start | bytes 2359300
  2.2 9.7 %all-to-all-start = ((f32[4,1,8]{2,1,0:T(1,128)}), f32[4,1,8]{2,1,0:T(1,128)S(1)}, u32[]{:S(2)}, u32[]{:S(2)}) async-start(f32[4,1,8]{2,1,0:T(1,128)} %broadcast_in_dim.17), calls=%async_computation | async-start | bytes 4096 | tf_op jit(solution)/shard_map/all_to_all | solution.py:15
  6.6 1.8 %copy-start.1 = (bf16[1,1536,256]{2,1,0:T(8,128)(2,1)S(1)}, bf16[1,1536,256]{2,1,0:T(8,128)(2,1)}, u32[]{:S(2)}) copy-start(bf16[1,1536,256]{2,1,0:T(8,128)(2,1)} %param.13) | copy-start | bytes 2359300
  6.6 1.8 %copy-start.4 = (bf16[1,640,256]{2,1,0:T(8,128)(2,1)S(1)}, bf16[1,640,256]{2,1,0:T(8,128)(2,1)}, u32[]{:S(2)}) copy-start(bf16[1,640,256]{2,1,0:T(8,128)(2,1)} %param.15) | copy-start | bytes 983044
  11.8 4.5 %copy-start.6 = (s32[8,2]{0,1:T(2,128)S(1)}, s32[8,2]{0,1:T(2,128)}, u32[]{:S(2)}) copy-start(s32[8,2]{0,1:T(2,128)} %param.10) | copy-start | bytes 196
  11.8 4.5 %copy-start.7 = (s32[8,2]{0,1:T(2,128)S(1)}, s32[8,2]{0,1:T(2,128)}, u32[]{:S(2)}) copy-start(s32[8,2]{0,1:T(2,128)} %param.11) | copy-start | bytes 196
  11.8 4.7 %copy-start.2 = (bf16[8,1536]{1,0:T(8,128)(2,1)S(1)}, bf16[8,1536]{1,0:T(8,128)(2,1)}, u32[]{:S(2)}) copy-start(bf16[8,1536]{1,0:T(8,128)(2,1)} %param.8) | copy-start | bytes 73732
  11.8 4.7 %copy-start.5 = (f32[1536]{0:T(1024)S(1)}, f32[1536]{0:T(1024)}, u32[]{:S(2)}) copy-start(f32[1536]{0:T(1024)} %param.9) | copy-start | bytes 18436
  11.8 27.9 %all-to-all-start.3 = ((bf16[4,160,1536]{2,1,0:T(8,128)(2,1)}), bf16[4,160,1536]{2,1,0:T(8,128)(2,1)S(1)}, u32[]{:S(2)}, u32[]{:S(2)}) async-start(bf16[4,160,1536]{2,1,0:T(8,128)(2,1)} %bitcast.31), calls=%async_computation.3 | async-start | bytes 3932160 | tf_op jit(solution)/shard_map/all_to_all | solution.py:15
  40.6 36.1 %all-to-all-start.1 = ((bf16[16,8,1664]{2,1,0:T(8,128)(2,1)}), bf16[16,8,1664]{2,1,0:T(8,128)(2,1)S(1)}, u32[]{:S(2)}, u32[]{:S(2)}) async-start(bf16[16,8,1664]{2,1,0:T(8,128)(2,1)} %broadcast_in_dim.18), calls=%async_computation.1 | async-start | bytes 851968 | tf_op jit(solution)/shard_map/all_to_all | solution.py:15
  57.0 21.5 %collective-permute-start.1 = (bf16[160,1536]{1,0:T(8,128)(2,1)}, bf16[160,1536]{1,0:T(8,128)(2,1)S(1)}, u32[]{:S(2)}, u32[]{:S(2)}) collective-permute-start(bf16[160,1536]{1,0:T(8,128)(2,1)} %reduce_sum.59), channel_id=1, source_target_pairs={{0,128},{128,0},{1,129},{129,1},{2,130},{130,2},{3,131},{131,3},{4... | collective-permute-start | bytes 1474568 | tf_op jit(solution)/shard_map/ppermute | solution.py:28
  79.5 29.4 %all-to-all-start.4 = ((bf16[16,8,1536]{2,1,0:T(8,128)(2,1)}), bf16[16,8,1536]{2,1,0:T(8,128)(2,1)S(1)}, u32[]{:S(2)}, u32[]{:S(2)}) async-start(bf16[16,8,1536]{2,1,0:T(8,128)(2,1)} %fusion.4), calls=%async_computation.4 | async-start | bytes 786432 | tf_op jit(solution)/shard_map/all_to_all | solution.py:15
  87.7 27.4 %collective-permute-start = (bf16[160,1536]{1,0:T(8,128)(2,1)S(1)}, bf16[160,1536]{1,0:T(8,128)(2,1)S(1)}, u32[]{:S(2)}, u32[]{:S(2)}) collective-permute-start(bf16[160,1536]{1,0:T(8,128)(2,1)S(1)} %convolution_convert_fusion.2), channel_id=1, source_target_pairs={{0,128},{128,0},{1,129},{129,1},{2,130},{130,2},{3,131},{131,3},{4... | collective-permute-start | bytes 1474568 | tf_op jit(solution)/shard_map/ppermute | solution.py:28
  109.8 10.5 %all-to-all-start.5 = ((f32[4,1,8]{2,1,0:T(1,128)}), f32[4,1,8]{2,1,0:T(1,128)S(1)}, u32[]{:S(2)}, u32[]{:S(2)}) async-start(f32[4,1,8]{2,1,0:T(1,128)} %broadcast_in_dim.23), calls=%async_computation.5 | async-start | bytes 4096 | tf_op jit(solution)/shard_map/all_to_all | solution.py:15
  121.7 25.0 %copy-start.3 = (bf16[1,640,256]{2,1,0:T(8,128)(2,1)S(1)}, bf16[1,640,256]{2,1,0:T(8,128)(2,1)}, u32[]{:S(2)}) copy-start(bf16[1,640,256]{2,1,0:T(8,128)(2,1)} %param.14) | copy-start | bytes 983044
  121.7 25.0 %all-to-all-start.2 = ((bf16[4,160,1536]{2,1,0:T(8,128)(2,1)}), bf16[4,160,1536]{2,1,0:T(8,128)(2,1)S(1)}, u32[]{:S(2)}, u32[]{:S(2)}) async-start(bf16[4,160,1536]{2,1,0:T(8,128)(2,1)} %broadcast_in_dim.20), calls=%async_computation.2 | async-start | bytes 3932160 | tf_op jit(solution)/shard_map/all_to_all | solution.py:15
